TPU v7x, 32 devices: a whole 2x2x4 slice. The times are simulated.
32 devices in a mesh: wide: 8 (over y, x, core), narrow: 4 (over z).
Axes of the slice: x: 2, y: 2, z: 4, core: 2. Of those that a mesh axis runs over, the one named last changes fastest.
Arguments:
- amplitudes: float32 [2, 8, 8, 4, 128, 128], P(None, None, 'wide', 'narrow'), may hold values from -6 to 6
- gates: float32 [3, 2, 2, 128, 128], replicated, may hold values from -0.375 to 0.375
Outputs:
- final_state: float32 [2, 8, 8, 4, 128, 128], P(None, None, 'wide', 'narrow')
All inputs are finite; a program needn't handle non-finite values.
Results may differ from a plain program's by a relative error of at most 0.0001.
Values sent between devices are 32-bit elements; how exact they have to be, the bound alone decides.
A program may use at most 64 MiB of HBM per device.

v0:
```python
import jax
import jax.numpy as jnp
from jax import lax
from jax.sharding import PartitionSpec as P

precise = lax.Precision.HIGHEST


def blocks(matrix):
    return jnp.stack([jnp.stack([matrix[0], -matrix[1]]), jnp.stack([matrix[1], matrix[0]])])


def on_rows(vector, matrix):
    return jnp.einsum("cdjk,drkb->crjb", blocks(matrix), vector, precision=precise)


def on_columns(vector, matrix):
    return jnp.einsum("cdjk,drak->craj", blocks(matrix), vector, precision=precise)


def shards(amplitudes, gates):
    layout = amplitudes.shape
    slab_count = layout[1]
    gate_order = layout[4]
    vector = amplitudes.reshape(2, slab_count, gate_order, gate_order)
    vector = on_rows(vector, gates[0, 0])
    vector = on_columns(vector, gates[0, 1])
    resident = vector.reshape(layout)
    arrived = lax.all_to_all(resident, "wide", split_axis=4, concat_axis=2, tiled=True)
    items_here = arrived.shape[1]
    slab_data = arrived.reshape(2, items_here, gate_order, gate_order)
    slab_data = on_rows(slab_data, gates[1, 0])
    slab_data = on_columns(slab_data, gates[1, 1])
    resident = slab_data.reshape(2, items_here, 1, 1, gate_order, gate_order)
    arrived = lax.all_to_all(resident, "narrow", split_axis=4, concat_axis=3, tiled=True)
    vector = arrived.reshape(2, slab_count, gate_order, gate_order)
    vector = on_rows(vector, gates[2, 0])
    vector = on_columns(vector, gates[2, 1])
    return vector.reshape(layout)


def solution(mesh):
    return jax.shard_map(
        shards,
        mesh=mesh,
        in_specs=(P(None, None, "wide", "narrow", None, None), P()),
        out_specs=P(None, None, "wide", "narrow", None, None),
        check_vma=False,
    )
```

profile of v0, /device:TPU:2, one launch (start us, length us, event | category | flops | bytes accessed | tf_op | source)
XLA Modules:
  0.0 62.3 jit_solution(2130488809126210702)
XLA Ops:
  0.0 0.0 copy-start
  0.0 0.0 copy-start.1
  0.0 1.3 %slice_bitcast_fusion = (f32[1,128,128]{2,1,0:T(8,128)S(1)}, f32[1,128,128]{2,1,0:T(8,128)S(1)}, f32[1,128,128]{2,1,0:T(8,128)S(1)}, f32[1,128,128]{2,1,0:T(8,12...) fusion(f32[3,2,2,128,128]{4,3,2,1,0:T(8,128)} %param.3), kind=kLoop, calls=%fused_computation.39 | loop fusion | bytes 1572864 | tf_op jit(solution)/shard_map/squeeze | solution.py:10
  1.3 0.2 copy-done.1
  1.6 0.2 copy-done
  1.8 1.0 %convolution_bitcast_fusion.5 = f32[2,8,128,128,1]{3,2,0,4,1:T(8,128)S(1)} fusion(f32[1,2,128,128]{3,2,1,0:T(8,128)S(1)} %get-tuple-element.34, f32[1,2,128,128]{3,2,1,0:T(8,128)S(1)} %get-tuple-element.33, f32[2,8,1,1,128,128]{5,4,3,2,1,0:T(8,128)S(1)} %copy-done), kind=kOutput, calls=%fused_computation.5 | convolution fusion | flops 805371904 | bytes 2359296 | tf_op jit(solution)/shard_map/cdjk,drkb->crjb/dot_general | solution.py:14
  2.8 1.0 %convolution_bitcast_fusion.4 = f32[2,8,1,1,128,128]{5,4,0,1,3,2:T(8,128)S(1)} fusion(f32[2,8,128,128,1]{3,2,0,4,1:T(8,128)S(1)} %convolution_bitcast_fusion.5, f32[1,2,128,128]{3,2,1,0:T(8,128)S(1)} %get-tuple-element.35, f32[1,2,128,128]{3,2,1,0:T(8,128)S(1)} %get-tuple-element.36), kind=kOutput, calls=%fused_computation.4 | convolution fusion | flops 805371904 | bytes 2359296 | tf_op jit(solution)/shard_map/cdjk,drak->craj/dot_general | solution.py:18
  3.9 1.8 %copy.4 = f32[2,8,1,1,128,128]{5,0,1,3,2,4:T(2,128)} copy(f32[2,8,1,1,128,128]{5,4,0,1,3,2:T(8,128)S(1)} %convolution_bitcast_fusion.4) | data formatting | bytes 2097152 | tf_op jit(solution)/shard_map/reshape | solution.py:28
  5.6 4.2 %all-to-all-start = ((f32[2,8,1,1,128,128]{5,0,1,3,2,4:T(2,128)}), f32[2,8,1,1,128,128]{5,0,1,3,2,4:T(2,128)S(1)}, u32[]{:S(2)}, u32[]{:S(2)}) async-start(f32[2,8,1,1,128,128]{5,0,1,3,2,4:T(2,128)} %copy.4), calls=%async_computation | async-start | bytes 2097152 | tf_op jit(solution)/shard_map/all_to_all | solution.py:29
  9.9 13.8 %all-to-all-done = f32[2,8,1,1,128,128]{5,0,1,3,2,4:T(2,128)S(1)} async-done(((f32[2,8,1,1,128,128]{5,0,1,3,2,4:T(2,128)}), f32[2,8,1,1,128,128]{5,0,1,3,2,4:T(2,128)S(1)}, u32[]{:S(2)}, u32[]{:S(2)}) %all-to-all-start) | async-done | bytes 1048608 | tf_op jit(solution)/shard_map/all_to_all | solution.py:29
  23.8 1.4 %convolution_bitcast_fusion.3 = f32[2,8,128,128,1]{3,2,0,4,1:T(8,128)S(1)} fusion(f32[2,8,128,128,1]{3,0,1,2,4:T(2,128)S(1)} %bitcast.142, f32[1,2,128,128]{3,2,1,0:T(8,128)S(1)} %get-tuple-element.30, f32[1,2,128,128]{3,2,1,0:T(8,128)S(1)} %get-tuple-element.29), kind=kOutput, calls=%fused_computation.3 | convolution fusion | flops 805371904 | bytes 2359296 | tf_op jit(solution)/shard_map/cdjk,drkb->crjb/dot_general | solution.py:14
  25.2 1.0 %convolution_bitcast_fusion.2 = f32[2,8,1,1,128,128]{5,4,0,1,3,2:T(8,128)S(1)} fusion(f32[2,8,128,128,1]{3,2,0,4,1:T(8,128)S(1)} %convolution_bitcast_fusion.3, f32[1,2,128,128]{3,2,1,0:T(8,128)S(1)} %get-tuple-element.37, f32[1,2,128,128]{3,2,1,0:T(8,128)S(1)} %get-tuple-element.38), kind=kOutput, calls=%fused_computation.2 | convolution fusion | flops 805371904 | bytes 2359296 | tf_op jit(solution)/shard_map/cdjk,drak->craj/dot_general | solution.py:18
  26.2 1.8 %copy.5 = f32[2,8,1,1,128,128]{5,0,1,3,2,4:T(2,128)} copy(f32[2,8,1,1,128,128]{5,4,0,1,3,2:T(8,128)S(1)} %convolution_bitcast_fusion.2) | data formatting | bytes 2097152 | tf_op jit(solution)/shard_map/reshape | solution.py:34
  28.0 4.9 %all-to-all-start.1 = ((f32[2,8,1,1,128,128]{5,0,1,3,2,4:T(2,128)}), f32[2,8,1,1,128,128]{5,0,1,3,2,4:T(2,128)S(1)}, u32[]{:S(2)}, u32[]{:S(2)}) async-start(f32[2,8,1,1,128,128]{5,0,1,3,2,4:T(2,128)} %copy.5), calls=%async_computation.1 | async-start | bytes 2097152 | tf_op jit(solution)/shard_map/all_to_all | solution.py:35
  32.9 25.9 %all-to-all-done.1 = f32[2,8,1,1,128,128]{5,0,1,3,2,4:T(2,128)S(1)} async-done(((f32[2,8,1,1,128,128]{5,0,1,3,2,4:T(2,128)}), f32[2,8,1,1,128,128]{5,0,1,3,2,4:T(2,128)S(1)}, u32[]{:S(2)}, u32[]{:S(2)}) %all-to-all-start.1) | async-done | bytes 1048608 | tf_op jit(solution)/shard_map/all_to_all | solution.py:35
  58.8 1.4 %convolution_bitcast_fusion.1 = f32[2,8,128,128,1]{3,2,0,4,1:T(8,128)S(1)} fusion(f32[2,8,128,128,1]{3,0,1,2,4:T(2,128)S(1)} %bitcast.141, f32[1,2,128,128]{3,2,1,0:T(8,128)S(1)} %get-tuple-element.26, f32[1,2,128,128]{3,2,1,0:T(8,128)S(1)} %get-tuple-element.25), kind=kOutput, calls=%fused_computation.1 | convolution fusion | flops 805371904 | bytes 2359296 | tf_op jit(solution)/shard_map/cdjk,drkb->crjb/dot_general | solution.py:14
  60.2 1.0 %convolution_bitcast_fusion = f32[2,8,1,1,128,128]{5,4,0,1,3,2:T(8,128)S(1)} fusion(f32[2,8,128,128,1]{3,2,0,4,1:T(8,128)S(1)} %convolution_bitcast_fusion.1, f32[1,2,128,128]{3,2,1,0:T(8,128)S(1)} %get-tuple-element.39, f32[1,2,128,128]{3,2,1,0:T(8,128)S(1)} %get-tuple-element.40), kind=kOutput, calls=%fused_computation | convolution fusion | flops 805371904 | bytes 2359296 | tf_op jit(solution)/shard_map/cdjk,drak->craj/dot_general | solution.py:18
  61.3 1.1 %copy.6 = f32[2,8,1,1,128,128]{5,4,3,2,1,0:T(8,128)} copy(f32[2,8,1,1,128,128]{5,4,0,1,3,2:T(8,128)S(1)} %convolution_bitcast_fusion) | data formatting | bytes 2097152 | tf_op jit(solution)/shard_map/reshape | solution.py:39
  (4 shorter events, 0.1 us)
Async XLA Ops:
  0.0 1.8 %copy-start = (f32[2,8,1,1,128,128]{5,4,3,2,1,0:T(8,128)S(1)}, f32[2,8,1,1,128,128]{5,4,3,2,1,0:T(8,128)}, u32[]{:S(2)}) copy-start(f32[2,8,1,1,128,128]{5,4,3,2,1,0:T(8,128)} %param.2) | copy-start | bytes 3145732
  0.0 1.5 %copy-start.1 = (f32[3,2,2,128,128]{4,3,2,1,0:T(8,128)S(1)}, f32[3,2,2,128,128]{4,3,2,1,0:T(8,128)}, u32[]{:S(2)}) copy-start(f32[3,2,2,128,128]{4,3,2,1,0:T(8,128)} %param.3) | copy-start | bytes 2359300
  5.6 18.1 %all-to-all-start = ((f32[2,8,1,1,128,128]{5,0,1,3,2,4:T(2,128)}), f32[2,8,1,1,128,128]{5,0,1,3,2,4:T(2,128)S(1)}, u32[]{:S(2)}, u32[]{:S(2)}) async-start(f32[2,8,1,1,128,128]{5,0,1,3,2,4:T(2,128)} %copy.4), calls=%async_computation | async-start | bytes 2097152 | tf_op jit(solution)/shard_map/all_to_all | solution.py:29
  28.0 30.8 %all-to-all-start.1 = ((f32[2,8,1,1,128,128]{5,0,1,3,2,4:T(2,128)}), f32[2,8,1,1,128,128]{5,0,1,3,2,4:T(2,128)S(1)}, u32[]{:S(2)}, u32[]{:S(2)}) async-start(f32[2,8,1,1,128,128]{5,0,1,3,2,4:T(2,128)} %copy.5), calls=%async_computation.1 | async-start | bytes 2097152 | tf_op jit(solution)/shard_map/all_to_all | solution.py:35
where the time goes:
time: 62.6 us; the launch traced here: 62.3 us
  waiting for transfers between devices  39.7 us (63%)
  starting transfers between devices  9.12 us (15%)
  matrix products  6.91 us (11%)
  local copies, waits for them, and re-layouts  6.33 us (10%)
    all_to_all x1, waiting for transfers between devices, shards(): lax.all_to_all(resident, 'narrow', split_axis=4, concat_axis=3, tiled=True)  25.9 us
    all_to_all x1, waiting for transfers between devices, shards(): lax.all_to_all(resident, 'wide', split_axis=4, concat_axis=2, tiled=True)  13.8 us
    all_to_all x1, starting transfers between devices, shards(): lax.all_to_all(resident, 'narrow', split_axis=4, concat_axis=3, tiled=True)  4.87 us
    all_to_all x1, starting transfers between devices, shards(): lax.all_to_all(resident, 'wide', split_axis=4, concat_axis=2, tiled=True)  4.25 us
    dot_general x3, matrix products, on_rows(): jnp.einsum('cdjk,drkb->crjb', blocks(matrix), vector, precision=precise)  3.83 us
    dot_general x3, matrix products, on_columns(): jnp.einsum('cdjk,drak->craj', blocks(matrix), vector, precision=precise)  3.08 us
    reshape x1, local copies, waits for them, and re-layouts, shards(): resident = vector.reshape(layout)  1.78 us
    reshape x1, local copies, waits for them, and re-layouts, shards(): resident = slab_data.reshape(2, items_here, 1, 1, gate_order, gate_order)  1.78 us
  transfers between devices with their start and end apart: 2, of which 2 were waited for; matrix products, arithmetic and copies ran while one was open for 0% of the time, Pallas kernels for 0%

commit v1 on v0

--- a/solution.py
+++ b/solution.py
@@ -26,7 +26,9 @@
     vector = on_rows(vector, gates[0, 0])
     vector = on_columns(vector, gates[0, 1])
     resident = vector.reshape(layout)
-    arrived = lax.all_to_all(resident, "wide", split_axis=4, concat_axis=2, tiled=True)
+    pieces = jnp.split(resident, lax.axis_size("wide"), axis=4)
+    received = lax.all_to_all(jnp.stack(pieces), "wide", 0, 0)
+    arrived = jnp.concatenate(received, axis=2)
     items_here = arrived.shape[1]
     slab_data = arrived.reshape(2, items_here, gate_order, gate_order)
     slab_data = on_rows(slab_data, gates[1, 0])

time: 62.6 us -> 69.3 us (1.11)
  local copies, waits for them, and re-layouts: 6.33 us -> 10.5 us
  matrix products: 6.91 us -> 9.42 us
    unnamed x4 -> x11, local copies, waits for them, and re-layouts: 0.37 us -> 5.02 us
    reshape x1, local copies, waits for them, and re-layouts: 1.78 us -> 0.1 us  [shards(): arrived = jnp.concatenate(received, axis=2)]
    dot_general x3, matrix products: 3.08 us -> 4.65 us  [on_columns(): jnp.einsum('cdjk,drak->craj', blocks(matrix), vector, precision=precise)]
    dot_general x3, matrix products: 3.83 us -> 4.76 us  [on_rows(): jnp.einsum('cdjk,drkb->crjb', blocks(matrix), vector, precision=precise)]
  transfers between devices with their start and end apart: 2 -> 2, of which waited for: 2 -> 2; matrix products, arithmetic and copies ran while one was open for 0% -> 1% of each run, Pallas kernels for 0% -> 0%
where the time goes in v1:
time: 69.3 us; the launch traced here: 69 us
  waiting for transfers between devices  39.1 us (56%)
  local copies, waits for them, and re-layouts  10.5 us (15%)
  matrix products  9.42 us (14%)
  starting transfers between devices  9.12 us (13%)
  other arithmetic  0.77 us (1%)
    all_to_all x1, waiting for transfers between devices, shards(): lax.all_to_all(resident, 'narrow', split_axis=4, concat_axis=3, tiled=True)  25.3 us
    all_to_all x1, waiting for transfers between devices, shards(): received = lax.all_to_all(jnp.stack(pieces), 'wide', 0, 0)  13.8 us
    unnamed x11, local copies, waits for them, and re-layouts  5.02 us
    all_to_all x1, starting transfers between devices, shards(): lax.all_to_all(resident, 'narrow', split_axis=4, concat_axis=3, tiled=True)  4.87 us
    dot_general x3, matrix products, on_rows(): jnp.einsum('cdjk,drkb->crjb', blocks(matrix), vector, precision=precise)  4.76 us
    dot_general x3, matrix products, on_columns(): jnp.einsum('cdjk,drak->craj', blocks(matrix), vector, precision=precise)  4.65 us
    all_to_all x1, starting transfers between devices, shards(): received = lax.all_to_all(jnp.stack(pieces), 'wide', 0, 0)  4.25 us
    reshape x1, local copies, waits for them, and re-layouts, shards(): resident = slab_data.reshape(2, items_here, 1, 1, gate_order, gate_order)  1.78 us
  transfers between devices with their start and end apart: 2, of which 2 were waited for; matrix products, arithmetic and copies ran while one was open for 1% of the time, Pallas kernels for 0%

profile of v1, /device:TPU:2, one launch (start us, length us, event | category | flops | bytes accessed | tf_op | source)
XLA Modules:
  0.0 69.0 jit_solution(16860409373474066038)
XLA Ops:
  0.0 1.3 %slice_bitcast_fusion.8 = (f32[1,128,128]{2,1,0:T(8,128)S(1)}, f32[1,128,128]{2,1,0:T(8,128)S(1)}, f32[1,128,128]{2,1,0:T(8,128)S(1)}, f32[1,128,128]{2,1,0:T(8,...) fusion(f32[3,2,2,128,128]{4,3,2,1,0:T(8,128)} %param.3), kind=kLoop, calls=%fused_computation.55 | loop fusion | bytes 1572864 | tf_op jit(solution)/shard_map/squeeze | solution.py:10
  1.3 0.2 copy-done.1
  1.8 1.0 %convolution_bitcast_fusion.5 = f32[2,8,128,128,1]{3,2,0,4,1:T(8,128)S(1)} fusion(f32[1,2,128,128]{3,2,1,0:T(8,128)S(1)} %get-tuple-element.34, f32[1,2,128,128]{3,2,1,0:T(8,128)S(1)} %get-tuple-element.33, f32[2,8,1,1,128,128]{5,4,3,2,1,0:T(8,128)S(1)} %copy-done), kind=kOutput, calls=%fused_computation.5 | convolution fusion | flops 805371904 | bytes 2359296 | tf_op jit(solution)/shard_map/cdjk,drkb->crjb/dot_general | solution.py:14
  2.8 1.0 %convolution_bitcast_fusion.4 = f32[2,8,1,1,128,128]{5,4,0,1,3,2:T(8,128)S(1)} fusion(f32[2,8,128,128,1]{3,2,0,4,1:T(8,128)S(1)} %convolution_bitcast_fusion.5, f32[1,2,128,128]{3,2,1,0:T(8,128)S(1)} %get-tuple-element.35, f32[1,2,128,128]{3,2,1,0:T(8,128)S(1)} %get-tuple-element.36), kind=kOutput, calls=%fused_computation.4 | convolution fusion | flops 805371904 | bytes 2359296 | tf_op jit(solution)/shard_map/cdjk,drak->craj/dot_general | solution.py:18
  3.9 0.7 fusion.22
  4.5 0.7 fusion.21
  5.2 0.7 fusion.20
  5.8 0.7 fusion.19
  6.5 0.7 fusion.18
  7.2 0.7 fusion.17
  7.8 0.7 fusion.16
  8.5 0.7 fusion.15
  9.2 4.2 %all-to-all-start = ((f32[8,2,8,1,1,16,128]{6,5,1,2,4,3,0:T(8,128)}), f32[8,2,8,1,1,16,128]{6,5,1,2,4,3,0:T(8,128)S(1)}, u32[]{:S(2)}, u32[]{:S(2)}) async-start(f32[8,2,8,1,1,16,128]{6,5,1,2,4,3,0:T(8,128)} %fusion.15), calls=%async_computation | async-start | bytes 2097152 | tf_op jit(solution)/shard_map/all_to_all | solution.py:30
  13.5 13.8 %all-to-all-done = f32[8,2,8,1,1,16,128]{6,5,1,2,4,3,0:T(8,128)S(1)} async-done(((f32[8,2,8,1,1,16,128]{6,5,1,2,4,3,0:T(8,128)}), f32[8,2,8,1,1,16,128]{6,5,1,2,4,3,0:T(8,128)S(1)}, u32[]{:S(2)}, u32[]{:S(2)}) %all-to-all-start) | async-done | bytes 1048608 | tf_op jit(solution)/shard_map/all_to_all | solution.py:30
  27.4 1.8 %convolution_bitcast_fusion.3 = f32[2,8,128,128,1]{2,3,0,4,1:T(8,128)S(1)} fusion(f32[2,8,128,128,1]{3,2,1,0,4:T(8,128)S(1)} %bitcast.179, f32[1,2,128,128]{3,2,1,0:T(8,128)S(1)} %get-tuple-element.30, f32[1,2,128,128]{3,2,1,0:T(8,128)S(1)} %get-tuple-element.29), kind=kOutput, calls=%fused_computation.3 | convolution fusion | flops 805371904 | bytes 2359296 | tf_op jit(solution)/shard_map/cdjk,drkb->crjb/dot_general | solution.py:14
  29.2 1.8 %convolution_bitcast_fusion.2 = f32[2,8,1,1,128,128]{5,4,0,1,3,2:T(8,128)S(1)} fusion(f32[2,8,128,128,1]{2,3,0,4,1:T(8,128)S(1)} %convolution_bitcast_fusion.3, f32[1,2,128,128]{3,2,1,0:T(8,128)S(1)} %get-tuple-element.28, f32[1,2,128,128]{3,2,1,0:T(8,128)S(1)} %get-tuple-element.27), kind=kOutput, calls=%fused_computation.2 | convolution fusion | flops 805371904 | bytes 2359296 | tf_op jit(solution)/shard_map/cdjk,drak->craj/dot_general | solution.py:18
  31.1 1.8 %copy.10 = f32[2,8,1,1,128,128]{5,0,1,3,2,4:T(2,128)} copy(f32[2,8,1,1,128,128]{5,4,0,1,3,2:T(8,128)S(1)} %convolution_bitcast_fusion.2) | data formatting | bytes 2097152 | tf_op jit(solution)/shard_map/reshape | solution.py:36
  32.8 4.9 %all-to-all-start.1 = ((f32[2,8,1,1,128,128]{5,0,1,3,2,4:T(2,128)}), f32[2,8,1,1,128,128]{5,0,1,3,2,4:T(2,128)S(1)}, u32[]{:S(2)}, u32[]{:S(2)}) async-start(f32[2,8,1,1,128,128]{5,0,1,3,2,4:T(2,128)} %copy.10), calls=%async_computation.1 | async-start | bytes 2097152 | tf_op jit(solution)/shard_map/all_to_all | solution.py:37
  37.7 0.7 maximum_bitcast_fusion.20
  38.4 25.3 %all-to-all-done.1 = f32[2,8,1,1,128,128]{5,0,1,3,2,4:T(2,128)S(1)} async-done(((f32[2,8,1,1,128,128]{5,0,1,3,2,4:T(2,128)}), f32[2,8,1,1,128,128]{5,0,1,3,2,4:T(2,128)S(1)}, u32[]{:S(2)}, u32[]{:S(2)}) %all-to-all-start.1) | async-done | bytes 1048608 | tf_op jit(solution)/shard_map/all_to_all | solution.py:37
  63.7 0.5 copy.11
  64.2 1.9 %convolution_bitcast_fusion.1 = f32[2,8,128,128,1]{2,3,0,4,1:T(8,128)S(1)} fusion(f32[2,8,1,1,128,128]{4,5,0,1,3,2:T(8,128)S(1)} %copy.11, f32[1,2,128,128]{3,2,1,0:T(8,128)} %get-tuple-element.26, f32[1,2,128,128]{3,2,1,0:T(8,128)S(1)} %get-tuple-element.25), kind=kOutput, calls=%fused_computation.1 | convolution fusion | flops 805371904 | bytes 2359296 | tf_op jit(solution)/shard_map/cdjk,drkb->crjb/dot_general | solution.py:14
  66.1 1.8 %convolution_bitcast_fusion = f32[2,8,1,1,128,128]{5,4,0,1,3,2:T(8,128)S(1)} fusion(f32[2,8,128,128,1]{2,3,0,4,1:T(8,128)S(1)} %convolution_bitcast_fusion.1, f32[1,2,128,128]{3,2,1,0:T(8,128)S(1)} %get-tuple-element.37, f32[1,2,128,128]{3,2,1,0:T(8,128)S(1)} %get-tuple-element.38), kind=kOutput, calls=%fused_computation | convolution fusion | flops 805371904 | bytes 2359296 | tf_op jit(solution)/shard_map/cdjk,drak->craj/dot_general | solution.py:18
  67.9 1.1 %copy.13 = f32[2,8,1,1,128,128]{5,4,3,2,1,0:T(8,128)} copy(f32[2,8,1,1,128,128]{5,4,0,1,3,2:T(8,128)S(1)} %convolution_bitcast_fusion) | data formatting | bytes 2097152 | tf_op jit(solution)/shard_map/reshape | solution.py:41
  (8 shorter events, 0.4 us)
Async XLA Ops:
  0.0 1.8 %copy-start = (f32[2,8,1,1,128,128]{5,4,3,2,1,0:T(8,128)S(1)}, f32[2,8,1,1,128,128]{5,4,3,2,1,0:T(8,128)}, u32[]{:S(2)}) copy-start(f32[2,8,1,1,128,128]{5,4,3,2,1,0:T(8,128)} %param.2) | copy-start | bytes 3145732
  0.0 1.5 %copy-start.1 = (f32[3,2,2,128,128]{4,3,2,1,0:T(8,128)S(1)}, f32[3,2,2,128,128]{4,3,2,1,0:T(8,128)}, u32[]{:S(2)}) copy-start(f32[3,2,2,128,128]{4,3,2,1,0:T(8,128)} %param.3) | copy-start | bytes 2359300
  9.2 18.1 %all-to-all-start = ((f32[8,2,8,1,1,16,128]{6,5,1,2,4,3,0:T(8,128)}), f32[8,2,8,1,1,16,128]{6,5,1,2,4,3,0:T(8,128)S(1)}, u32[]{:S(2)}, u32[]{:S(2)}) async-start(f32[8,2,8,1,1,16,128]{6,5,1,2,4,3,0:T(8,128)} %fusion.15), calls=%async_computation | async-start | bytes 2097152 | tf_op jit(solution)/shard_map/all_to_all | solution.py:30
  32.8 30.8 %all-to-all-start.1 = ((f32[2,8,1,1,128,128]{5,0,1,3,2,4:T(2,128)}), f32[2,8,1,1,128,128]{5,0,1,3,2,4:T(2,128)S(1)}, u32[]{:S(2)}, u32[]{:S(2)}) async-start(f32[2,8,1,1,128,128]{5,0,1,3,2,4:T(2,128)} %copy.10), calls=%async_computation.1 | async-start | bytes 2097152 | tf_op jit(solution)/shard_map/all_to_all | solution.py:37
